TPU v7x, 512 devices: a whole 4x8x8 slice. The times are simulated.
512 devices in a mesh: section: 8 (over y), dp: 16 (over z, core), tensor: 4 (over x).
Axes of the slice: x: 4, y: 8, z: 8, core: 2. Of those that a mesh axis runs over, the one named last changes fastest.
Arguments:
- section_inputs: bfloat16 [8, 128, 2560], P('section', 'dp', 'tensor'), may hold values from -40 to 40
- entering: bfloat16 [1, 128, 2560], P(None, 'dp', 'tensor'), may hold values from -40 to 40
- grad_outputs: bfloat16 [8, 128, 2560], P('section', 'dp', 'tensor'), may hold values from -6 to 6
- arriving: bfloat16 [1, 128, 2560], P(None, 'dp', 'tensor'), may hold values from -6 to 6
- live_rows: int32 [1], replicated, may hold values from 64 to 128
- stashed_inputs: bfloat16 [8, 2, 128, 2560], P('section', None, 'dp', 'tensor'), may hold values from -40 to 40
- norm_gain: bfloat16 [8, 2560], P('section', 'tensor'), may hold values from 0.25 to 1.75
- up_weight: bfloat16 [8, 2560, 14336], P('section', 'tensor', 'dp'), may hold values from -0.125 to 0.125
- down_weight: bfloat16 [8, 14336, 2560], P('section', 'dp', 'tensor'), may hold values from -0.046875 to 0.046875
- held_blocks: int32 [8, 4, 16, 6], P('section', 'tensor'), may hold values from 0 to 69, as said below
- held_count: int32 [8, 4, 16], P('section', 'tensor'), may hold values from 1 to 6, as said below
- held_owner: int32 [8, 4, 16, 6], P('section', 'tensor'), may hold values from 0 to 15, as said below
- first_moment: float32 [8, 4, 16, 6, 128, 128], P('section', 'tensor', 'dp'), may hold values from -4 to 4
- second_moment: float32 [8, 4, 16, 6, 128, 128], P('section', 'tensor', 'dp'), may hold values from 0.01 to 1
Outputs:
- section_outputs: bfloat16 [8, 2, 128, 2560], P('section', None, 'dp', 'tensor')
- input_grads: bfloat16 [8, 2, 128, 2560], P('section', None, 'dp', 'tensor')
- first_next: float32 [8, 4, 16, 6, 128, 128], P('section', 'tensor', 'dp')
- second_next: float32 [8, 4, 16, 6, 128, 128], P('section', 'tensor', 'dp')
- update_direction: float32 [8, 4, 16, 6, 128, 128], P('section', 'tensor', 'dp')
Inputs may be any that keep to these rules, and one draw needn't show every extreme that they name: `held_blocks`: A number below 35 names a block of the device's up projection share, row-major over 5 x 7 blocks; the others, less 35, a block of its down projection share, row-major over 7 x 5 blocks. A device's first held_count entries are distinct; later entries are not used. `held_count`: some device of each section and tensor index lists 6 trainable blocks. `held_owner`: the owners of one device's trainable blocks are distinct and never the device itself. Each dp index owns at most 6 blocks of one section and tensor index, and some owns exactly 6.
All inputs are finite; a program needn't handle non-finite values.
Results may differ from a plain program's by a relative error of at most 0.015.
Values may be sent and summed in bfloat16 or wider, within the bound.
A program may use at most 64 MiB of HBM per device.

v0:
```python
import jax
import jax.numpy as jnp
from jax import lax
from jax.sharding import PartitionSpec as P

DW = 2560
BLK = 128
EPSILON = 1e-06


def from_behind(value, axis, steps):
    count = lax.axis_size(axis)
    leading, last = (max(0, -steps), min(count, count - steps))
    return lax.ppermute(value, axis, [(source, source + steps) for source in range(leading, last)])


def normed_product(rows_all, gain_row, up_matrix):
    widened = rows_all.astype(jnp.float32)
    squares = jnp.sum(widened * widened, axis=1)
    normed = (widened * gain_row.astype(jnp.float32)).astype(jnp.bfloat16)
    product = jnp.dot(normed, up_matrix, preferred_element_type=jnp.float32)
    return (normed, squares, product)


def scales_of(squares):
    return lax.rsqrt(squares / DW + EPSILON)


def activate(hidden):
    return (hidden * jax.nn.sigmoid(hidden)).astype(jnp.bfloat16)


def hidden_backward(hidden, act_grad, row_scales, product):
    sigmoid_part = jax.nn.sigmoid(hidden)
    hidden_grad = act_grad * sigmoid_part * (1.0 + hidden * (1.0 - sigmoid_part))
    scaled_grad = (hidden_grad * row_scales[:, None]).astype(jnp.bfloat16)
    scale_grad = jnp.sum(hidden_grad * product, axis=1)
    return (scaled_grad, scale_grad)


def times_transposed(left, right):
    return lax.dot_general(
        left, right, (((1,), (1,)), ((), ())), preferred_element_type=jnp.float32
    )


def body(
    section_inputs,
    entering,
    grad_outputs,
    arriving,
    live_rows,
    stashed_inputs,
    norm_gain,
    up_weight,
    down_weight,
    held_blocks,
    held_count,
    held_owner,
    first_moment,
    second_moment,
):
    section_count = lax.axis_size("section")
    section_index = lax.axis_index("section")
    dp_index = lax.axis_index("dp")
    dp_count = lax.axis_size("dp")
    turn_count = stashed_inputs.shape[1]
    local_rows = section_inputs.shape[1]
    row_total = local_rows * dp_count
    gain_row = norm_gain[0]
    up_matrix = up_weight[0]
    down_matrix = down_weight[0]
    channel_blocks = up_matrix.shape[0] // BLK
    hidden_blocks = up_matrix.shape[1] // BLK
    up_count = channel_blocks * hidden_blocks
    capacity = held_owner.shape[3]
    row_start = dp_index * local_rows
    held_list = lax.dynamic_index_in_dim(held_blocks[0, 0], dp_index, 0, keepdims=False)
    down_number = held_list - up_count
    is_up = held_list < up_count
    left_index = jnp.where(
        is_up, held_list // hidden_blocks, channel_blocks + down_number // channel_blocks
    )
    right_index = jnp.where(
        is_up, held_list % hidden_blocks, hidden_blocks + down_number % channel_blocks
    )
    forward_results = []
    rows_in = section_inputs[0]
    for turn in range(turn_count):
        if turn > 0:
            passed_rows = from_behind(forward_results[-1], "section", 1)
            rows_in = jnp.where(section_index == 0, entering[turn - 1], passed_rows)
        forward_rows_all = lax.all_gather(rows_in, "dp", axis=0, tiled=True)
        forward_normed, forward_squares, forward_product = normed_product(
            forward_rows_all, gain_row, up_matrix
        )
        forward_product, forward_squares = (
            lax.psum(forward_product.astype(jnp.bfloat16), "tensor").astype(jnp.float32),
            lax.psum(forward_squares.astype(jnp.bfloat16), "tensor").astype(jnp.float32),
        )
        forward_activated = activate(forward_product * scales_of(forward_squares)[:, None])
        mixed_rows = lax.psum_scatter(
            jnp.dot(forward_activated, down_matrix, preferred_element_type=jnp.float32).astype(
                jnp.bfloat16
            ),
            "dp",
            scatter_dimension=0,
            tiled=True,
        ).astype(jnp.float32)
        forward_results.append((rows_in.astype(jnp.float32) + mixed_rows).astype(jnp.bfloat16))
    row_ids = row_start + lax.iota(jnp.int32, local_rows)
    backward_results = []
    kept_grads = jnp.zeros((capacity, BLK, BLK), jnp.float32)
    grads_in = grad_outputs[0]
    for turn in range(turn_count):
        if turn > 0:
            passed_grads = from_behind(backward_results[-1], "section", -1)
            masked = jnp.where(
                (row_ids < live_rows[turn - 1])[:, None],
                arriving[turn - 1],
                jnp.zeros_like(arriving[turn - 1]),
            )
            grads_in = jnp.where(section_index == section_count - 1, masked, passed_grads)
        rows_local = stashed_inputs[0, turn]
        rows_all = lax.all_gather(rows_local, "dp", axis=0, tiled=True)
        grads_all = lax.all_gather(grads_in, "dp", axis=0, tiled=True)
        normed, squares, product = normed_product(rows_all, gain_row, up_matrix)
        act_grad = times_transposed(grads_all, down_matrix)
        product, squares, act_grad = lax.psum((product, squares, act_grad), "tensor")
        row_scales = scales_of(squares)
        hidden = product * row_scales[:, None]
        activated = activate(hidden)
        scaled_grad, scale_grad = hidden_backward(hidden, act_grad, row_scales, product)
        normed_part = times_transposed(scaled_grad, up_matrix)
        normed_grad = lax.psum_scatter(normed_part, "dp", scatter_dimension=0, tiled=True)
        scale_grad_rows = lax.psum_scatter(scale_grad, "dp", scatter_dimension=0, tiled=True)
        scale_rows = lax.dynamic_slice_in_dim(row_scales, row_start, local_rows, 0)
        widened = rows_local.astype(jnp.float32)
        input_grad = (
            grads_in.astype(jnp.float32)
            + normed_grad * gain_row.astype(jnp.float32)
            - (scale_grad_rows * scale_rows**3)[:, None] * widened / DW
        )
        left_table = jnp.concatenate(
            [
                normed.reshape(row_total, channel_blocks, BLK),
                activated.reshape(row_total, hidden_blocks, BLK),
            ],
            axis=1,
        )
        right_table = jnp.concatenate(
            [
                scaled_grad.reshape(row_total, hidden_blocks, BLK),
                grads_all.reshape(row_total, channel_blocks, BLK),
            ],
            axis=1,
        )
        left_pick = jnp.take(left_table, left_index, axis=1)
        right_pick = jnp.take(right_table, right_index, axis=1)
        block_grads = jnp.einsum(
            "rkb,rkc->kbc", left_pick, right_pick, preferred_element_type=jnp.float32
        )
        result, block_grads = (input_grad.astype(jnp.bfloat16), block_grads)
        backward_results.append(result)
        kept_grads = kept_grads + block_grads
    counts = held_count[0, 0]
    owners = held_owner[0, 0]
    slot_ids = lax.iota(jnp.int32, capacity)
    dp_ids = lax.iota(jnp.int32, dp_count)
    live_slots = slot_ids[None, :] < counts[:, None]
    chosen = (owners[:, None, :] == dp_ids[None, :, None]) & live_slots[:, None, :]
    is_sent = jnp.any(chosen, axis=2)
    slot_pick = jnp.sum(jnp.where(chosen, slot_ids[None, None, :], 0), axis=2)
    mine_sent = lax.dynamic_index_in_dim(is_sent, dp_index, 0, keepdims=False)
    mine_pick = lax.dynamic_index_in_dim(slot_pick, dp_index, 0, keepdims=False)
    outgoing = jnp.where(mine_sent[:, None, None], jnp.take(kept_grads, mine_pick, axis=0), 0.0)
    arrived = lax.all_to_all(outgoing, "dp", split_axis=0, concat_axis=0, tiled=True)
    from_source = lax.dynamic_index_in_dim(is_sent, dp_index, 1, keepdims=False)
    source_count = from_source.astype(jnp.int32)
    ranks = jnp.cumsum(source_count) - source_count
    matches = from_source[None, :] & (ranks[None, :] == slot_ids[:, None])
    is_filled = jnp.any(matches, axis=1)
    source_ids = jnp.sum(jnp.where(matches, dp_ids[None, :], 0), axis=1)
    owned_grads = jnp.where(is_filled[:, None, None], jnp.take(arrived, source_ids, axis=0), 0.0)
    filled = is_filled[:, None, None]
    first_new = 0.9 * first_moment[0, 0, 0] + 0.1 * owned_grads
    second_new = 0.999 * second_moment[0, 0, 0] + 0.001 * owned_grads * owned_grads
    direction = first_new / (jnp.sqrt(second_new) + 1e-08)
    first_out = jnp.where(filled, first_new, 0.0)
    second_out = jnp.where(filled, second_new, 0.0)
    direction_out = jnp.where(filled, direction, 0.0)
    section_rows = jnp.stack(forward_results)
    grad_rows = jnp.stack(backward_results)
    return (
        section_rows[None],
        grad_rows[None],
        first_out[None, None, None],
        second_out[None, None, None],
        direction_out[None, None, None],
    )


def solution(mesh):
    return jax.shard_map(
        body,
        mesh=mesh,
        in_specs=(
            P("section", "dp", "tensor"),
            P(None, "dp", "tensor"),
            P("section", "dp", "tensor"),
            P(None, "dp", "tensor"),
            P(),
            P("section", None, "dp", "tensor"),
            P("section", "tensor"),
            P("section", "tensor", "dp"),
            P("section", "dp", "tensor"),
            P("section", "tensor", None, None),
            P("section", "tensor", None),
            P("section", "tensor", None, None),
            P("section", "tensor", "dp", None, None, None),
            P("section", "tensor", "dp", None, None, None),
        ),
        out_specs=(
            P("section", None, "dp", "tensor"),
            P("section", None, "dp", "tensor"),
            P("section", "tensor", "dp", None, None, None),
            P("section", "tensor", "dp", None, None, None),
            P("section", "tensor", "dp", None, None, None),
        ),
        check_vma=False,
    )
```

profile of v0, /device:TPU:1, one launch (start us, length us, event | category | flops | bytes accessed | tf_op | source)
XLA Modules:
  0.0 778.5 jit_solution(2961250332882547614)
XLA Ops:
  7.2 0.8 convert_reduce_fusion
  8.1 0.7 fusion.77
  8.8 24.9 %all-gather.2 = bf16[1,1,128,640]{3,2,1,0:T(8,128)(2,1)S(1)} all-gather(bf16[1,1,8,640]{3,2,1,0:T(8,128)(2,1)S(1)} %get-tuple-element.41), channel_id=4, replica_groups=mesh['section'=8,'dp'=16,'tensor'=4] {'dp'}, dimensions={2}, use_global_device_ids=true | all-gather | bytes 174080 | tf_op jit(solution)/shard_map/all_gather | solution.py:125
  33.9 15.2 %all-gather.1 = bf16[1,128,640]{2,1,0:T(8,128)(2,1)S(1)} all-gather(bf16[1,8,640]{2,1,0:T(8,128)(2,1)} %param.18), channel_id=3, replica_groups=mesh['section'=8,'dp'=16,'tensor'=4] {'dp'}, dimensions={1}, use_global_device_ids=true | all-gather | bytes 174080 | tf_op jit(solution)/shard_map/all_gather | solution.py:126
  49.0 16.2 %all-gather.3 = bf16[1,1,128,640]{3,2,1,0:T(8,128)(2,1)S(1)} all-gather(bf16[1,1,8,640]{3,2,1,0:T(8,128)(2,1)S(1)} %get-tuple-element.42), channel_id=5, replica_groups=mesh['section'=8,'dp'=16,'tensor'=4] {'dp'}, dimensions={2}, use_global_device_ids=true | all-gather | bytes 174080 | tf_op jit(solution)/shard_map/all_gather | solution.py:125
  65.4 1.2 fusion.2
  66.8 1.2 fusion.12
  68.1 14.9 %all-gather = bf16[1,128,640]{2,1,0:T(8,128)(2,1)S(1)} all-gather(bf16[1,8,640]{2,1,0:T(8,128)(2,1)S(1)} %copy-done.15), channel_id=2, replica_groups=mesh['section'=8,'dp'=16,'tensor'=4] {'dp'}, dimensions={1}, use_global_device_ids=true | all-gather | bytes 174080 | tf_op jit(solution)/shard_map/all_gather | solution.py:93
  83.2 8.9 %all-reduce.6 = (f32[128]{0:T(128)S(1)}, f32[128]{0:T(128)S(1)}) all-reduce(f32[128]{0:T(128)S(1)} %get-tuple-element.38, f32[128]{0:T(128)S(1)} %get-tuple-element.43), channel_id=1, replica_groups=mesh['section'=8,'dp'=16,'tensor'=4] {'tensor'}, use_global_device_ids=true, to_apply=%region_18.19 | all-reduce | flops 256 | bytes 2048 | tf_op jit(solution)/shard_map/psum | solution.py:129
  92.1 27.8 %all-reduce.32.cloned.1.call-done = (f32[128,896]{1,0:T(8,128)}, f32[128,896]{1,0:T(8,128)}) async-done(((f32[128,896]{1,0:T(8,128)}, f32[128,896]{1,0:T(8,128)}), (f32[128,896]{1,0:T(8,128)}, f32[128,896]{1,0:T(8,128)})) %all-reduce.32.cloned.1.call-update) | async-done | bytes 917520 | tf_op jit(solution)/shard_map/psum | solution.py:129
  119.9 1.6 multiply_reduce_fusion.1
  121.4 1.2 fusion.10
  122.7 1.3 convolution_convert_fusion.1
  124.6 0.6 divide_reduce_fusion.1
  126.4 0.6 fusion.65
  129.6 8.1 %psum.71 = bf16[128]{0:T(256)(128)(2,1)S(1)} all-reduce(bf16[128]{0:T(256)(128)(2,1)S(1)} %fusion.21), channel_id=1, replica_groups=mesh['section'=8,'dp'=16,'tensor'=4] {'tensor'}, use_global_device_ids=true, to_apply=%region_2.3 | all-reduce | flops 128 | bytes 512 | tf_op jit(solution)/shard_map/psum | solution.py:99
  137.6 1.2 fusion.8
  138.8 1.3 dynamic-slice.1
  140.8 28.0 %all-reduce.3 = f32[128]{0:T(128)S(1)} all-reduce(f32[128]{0:T(128)S(1)} %get-tuple-element.30), channel_id=9, replica_groups=mesh['section'=8,'dp'=16,'tensor'=4] {'dp'}, use_global_device_ids=true, to_apply=%region_14.15.clone | all-reduce | flops 128 | bytes 1024
  168.9 69.6 %all-reduce.26.cloned.1.call-done = f32[128,640]{1,0:T(8,128)} async-done(((f32[128,640]{1,0:T(8,128)}), f32[128,640]{1,0:T(8,128)}) %all-reduce.26.cloned.1.call-update) | async-done | bytes 327696
  238.6 0.8 fusion.58
  239.4 1.4 collective-permute-start.1
  240.8 50.0 %all-reduce.18.cloned.1.call-done = bf16[128,896]{1,0:T(8,128)(2,1)} async-done(((bf16[128,896]{1,0:T(8,128)(2,1)}), bf16[128,896]{1,0:T(8,128)(2,1)}) %all-reduce.18.cloned.1.call-update) | async-done | bytes 229392 | tf_op jit(solution)/shard_map/psum | solution.py:98
  290.8 2.0 convolution_convert_fusion.3
  293.0 21.1 %all_gather.22 = bf16[128,640]{1,0:T(8,128)(2,1)S(1)} all-gather(bf16[8,640]{1,0:T(8,128)(2,1)S(1)} %fusion.63), channel_id=1, replica_groups=mesh['section'=8,'dp'=16,'tensor'=4] {'dp'}, dimensions={0}, use_global_device_ids=true | all-gather | bytes 174080 | tf_op jit(solution)/shard_map/all_gather | solution.py:126
  314.1 0.7 copy-done.2
  314.8 1.3 fusion
  316.0 88.5 %all-reduce.22.cloned.1.call-done = bf16[128,640]{1,0:T(8,128)(2,1)} async-done(((bf16[128,640]{1,0:T(8,128)(2,1)}), bf16[128,640]{1,0:T(8,128)(2,1)}) %all-reduce.22.cloned.1.call-update) | async-done | bytes 163856
  404.6 0.7 fusion.59
  405.3 3.1 collective-permute-start
  409.1 0.8 copy.104
  410.0 0.8 copy.99
  410.8 0.8 copy.107
  411.6 16.2 %all_gather.19 = bf16[128,640]{1,0:T(8,128)(2,1)S(1)} all-gather(bf16[8,640]{1,0:T(8,128)(2,1)S(1)} %bitcast_select_fusion.2), channel_id=1, replica_groups=mesh['section'=8,'dp'=16,'tensor'=4] {'dp'}, dimensions={0}, use_global_device_ids=true | all-gather | bytes 174080 | tf_op jit(solution)/shard_map/all_gather | solution.py:93
  428.4 0.8 copy.100
  429.4 1.1 pad_maximum_fusion
  431.1 1.0 pad_maximum_fusion.1
  433.2 0.8 copy.112
  434.0 26.0 %all-reduce.30.cloned.1.call-done = (f32[128,896]{1,0:T(8,128)}, f32[128,896]{1,0:T(8,128)}) async-done(((f32[128,896]{1,0:T(8,128)}, f32[128,896]{1,0:T(8,128)}), (f32[128,896]{1,0:T(8,128)}, f32[128,896]{1,0:T(8,128)})) %all-reduce.30.cloned.1.call-update) | async-done | bytes 917520 | tf_op jit(solution)/shard_map/psum | solution.py:129
  460.1 2.1 multiply_reduce_fusion
  462.4 0.8 copy.108
  463.2 1.1 pad_maximum_fusion.2
  464.3 1.4 gather_fusion.4
  465.8 0.8 copy.111
  466.7 1.1 pad_maximum_fusion.3
  467.7 1.4 gather_fusion.5
  469.1 1.4 convolution_add_fusion
  470.5 1.8 gather_fusion
  472.3 2.5 select_select_fusion
  474.7 9.7 %all-to-all-start = ((f32[16,128,128]{2,1,0:T(8,128)}), f32[16,128,128]{2,1,0:T(8,128)}, u32[]{:S(2)}, u32[]{:S(2)}) async-start(f32[16,128,128]{2,1,0:T(8,128)} %select_select_fusion), calls=%async_computation | async-start | bytes 2097152 | tf_op jit(solution)/shard_map/all_to_all | solution.py:177
  484.5 1.3 convolution_convert_fusion
  485.9 8.5 %psum.73 = bf16[128]{0:T(256)(128)(2,1)S(1)} all-reduce(bf16[128]{0:T(256)(128)(2,1)S(1)} %fusion.19), channel_id=1, replica_groups=mesh['section'=8,'dp'=16,'tensor'=4] {'tensor'}, use_global_device_ids=true, to_apply=%region_6.7 | all-reduce | flops 128 | bytes 512 | tf_op jit(solution)/shard_map/psum | solution.py:99
  494.4 43.6 %all-reduce.20.cloned.1.call-done = bf16[128,896]{1,0:T(8,128)(2,1)} async-done(((bf16[128,896]{1,0:T(8,128)(2,1)}), bf16[128,896]{1,0:T(8,128)(2,1)}) %all-reduce.20.cloned.1.call-update) | async-done | bytes 229392 | tf_op jit(solution)/shard_map/psum | solution.py:98
  538.1 2.0 convolution_convert_fusion.2
  540.2 111.8 %all-reduce.24.cloned.1.call-done = bf16[128,640]{1,0:T(8,128)(2,1)} async-done(((bf16[128,640]{1,0:T(8,128)(2,1)}), bf16[128,640]{1,0:T(8,128)(2,1)}) %all-reduce.24.cloned.1.call-update) | async-done | bytes 163856
  652.0 0.7 fusion.61
  652.7 1.2 fusion.6
  654.0 0.6 maximum_bitcast_fusion
  654.6 23.2 %all-reduce.5 = f32[128]{0:T(128)S(1)} all-reduce(f32[128]{0:T(128)S(1)} %copy-done.28), channel_id=11, replica_groups=mesh['section'=8,'dp'=16,'tensor'=4] {'dp'}, use_global_device_ids=true, to_apply=%region_21.22.clone | all-reduce | flops 128 | bytes 1024
  677.8 89.3 %all-reduce.28.cloned.1.call-done = f32[128,640]{1,0:T(8,128)} async-done(((f32[128,640]{1,0:T(8,128)}), f32[128,640]{1,0:T(8,128)}) %all-reduce.28.cloned.1.call-update) | async-done | bytes 327696
  767.1 0.8 fusion.62
  767.9 0.6 maximum_bitcast_fusion.1
  768.5 1.8 gather_fusion.1
  770.4 1.3 divide_select_fusion
  (133 shorter events, 8.7 us)
Async XLA Ops:
  7.2 59.6 %copy-start = (bf16[1,640,896]{2,1,0:T(8,128)(2,1)S(1)}, bf16[1,640,896]{2,1,0:T(8,128)(2,1)}, u32[]{:S(2)}) copy-start(bf16[1,640,896]{2,1,0:T(8,128)(2,1)} %param.23) | copy-start | bytes 3440644
  7.2 58.2 %copy-start.1 = (bf16[1,896,640]{2,1,0:T(8,128)(2,1)S(1)}, bf16[1,896,640]{2,1,0:T(8,128)(2,1)}, u32[]{:S(2)}) copy-start(bf16[1,896,640]{2,1,0:T(8,128)(2,1)} %param.24) | copy-start | bytes 3440644
  7.2 112.7 %all-reduce.32.cloned.1.call-start = ((), (), s32[]{:S(2)}) async-start(), calls=%async_computation.8 | async-start | bytes 1835008 | tf_op jit(solution)/shard_map/psum | solution.py:129
  66.8 1.3 copy-start.15
  68.0 170.5 %all-reduce.26.cloned.1.call-start = ((), (), s32[]{:S(2)}) async-start(), calls=%async_computation.5 | async-start | bytes 655360
  122.6 1.4 copy-start.16
  122.6 2.5 copy-start.34
  122.6 2.6 copy-start.25
  122.7 168.1 %all-reduce.18.cloned.1.call-start = ((), (), s32[]{:S(2)}) async-start(), calls=%async_computation.1 | async-start | bytes 458752 | tf_op jit(solution)/shard_map/psum | solution.py:98
  124.0 114.6 %copy-start.8 = (bf16[1,2,8,640]{3,2,1,0:T(8,128)(2,1)S(1)}, bf16[1,2,8,640]{3,2,1,0:T(8,128)(2,1)}, u32[]{:S(2)}) copy-start(bf16[1,2,8,640]{3,2,1,0:T(8,128)(2,1)} %param.21) | copy-start | bytes 61444
  124.0 114.6 %copy-start.14 = (bf16[1,8,640]{2,1,0:T(8,128)(2,1)S(1)}, bf16[1,8,640]{2,1,0:T(8,128)(2,1)}, u32[]{:S(2)}) copy-start(bf16[1,8,640]{2,1,0:T(8,128)(2,1)} %param.18) | copy-start | bytes 30724
  124.0 280.6 %all-reduce.22.cloned.1.call-start = ((), (), s32[]{:S(2)}) async-start(), calls=%async_computation.3 | async-start | bytes 327680
  129.6 330.5 %copy-start.26 = (f32[128]{0:T(128)}, f32[128]{0:T(128)S(1)}, u32[]{:S(2)}) copy-start(f32[128]{0:T(128)S(1)} %add_rsqrt_fusion) | copy-start | bytes 1540
  140.8 291.9 %copy-start.21 = (pred[6]{0:T(512)(128)(4,1)}, pred[6]{0:T(512)(128)(4,1)S(1)}, u32[]{:S(2)}) copy-start(pred[6]{0:T(512)(128)(4,1)S(1)} %get-tuple-element.24) | copy-start | bytes 22
  140.8 291.9 %copy-start.23 = (pred[6]{0:T(512)(128)(4,1)}, pred[6]{0:T(512)(128)(4,1)S(1)}, u32[]{:S(2)}) copy-start(pred[6]{0:T(512)(128)(4,1)S(1)} %get-tuple-element.47) | copy-start | bytes 22
  140.8 289.7 %copy-start.20 = (s32[1024]{0:T(1024)}, s32[1024]{0:T(1024)S(1)}, u32[]{:S(2)}) copy-start(s32[1024]{0:T(1024)S(1)} %get-tuple-element.50) | copy-start | bytes 12292
  140.8 291.3 %copy-start.19 = (s32[1024]{0:T(1024)}, s32[1024]{0:T(1024)S(1)}, u32[]{:S(2)}) copy-start(s32[1024]{0:T(1024)S(1)} %get-tuple-element.49) | copy-start | bytes 12292
  239.4 53.5 %copy-start.10 = (bf16[8,640]{1,0:T(8,128)(2,1)}, bf16[8,640]{1,0:T(8,128)(2,1)S(1)}, u32[]{:S(2)}) copy-start(bf16[8,640]{1,0:T(8,128)(2,1)S(1)} %fusion.58) | copy-start | bytes 30724
  239.4 53.5 %copy-start.17 = (bf16[1,8,640]{2,1,0:T(8,128)(2,1)S(1)}, bf16[1,8,640]{2,1,0:T(8,128)(2,1)}, u32[]{:S(2)}) copy-start(bf16[1,8,640]{2,1,0:T(8,128)(2,1)} %param.19) | copy-start | bytes 30724
  239.4 53.5 %collective-permute-start.1 = (bf16[8,640]{1,0:T(8,128)(2,1)S(1)}, bf16[8,640]{1,0:T(8,128)(2,1)S(1)}, u32[]{:S(2)}, u32[]{:S(2)}) collective-permute-start(bf16[8,640]{1,0:T(8,128)(2,1)S(1)} %fusion.58), channel_id=1, source_target_pairs={{64,0},{128,64},{192,128},{256,192},{320,256},{384,320},{448,384},... | collective-permute-start | bytes 30728 | tf_op jit(solution)/shard_map/ppermute | solution.py:14
  292.8 167.2 %all-reduce.30.cloned.1.call-start = ((), (), s32[]{:S(2)}) async-start(), calls=%async_computation.7 | async-start | bytes 1835008 | tf_op jit(solution)/shard_map/psum | solution.py:129
  314.1 0.7 copy-start.2
  316.0 95.6 %copy-start.18 = (bf16[1,8,640]{2,1,0:T(8,128)(2,1)S(1)}, bf16[1,8,640]{2,1,0:T(8,128)(2,1)}, u32[]{:S(2)}) copy-start(bf16[1,8,640]{2,1,0:T(8,128)(2,1)} %param.17) | copy-start | bytes 30724
  405.3 6.3 copy-start.12
  405.3 6.3 collective-permute-start
  411.6 17.6 %copy-start.6 = (bf16[8,640]{1,0:T(8,128)(2,1)}, bf16[8,640]{1,0:T(8,128)(2,1)S(1)}, u32[]{:S(2)}) copy-start(bf16[8,640]{1,0:T(8,128)(2,1)S(1)} %bitcast_select_fusion.2) | copy-start | bytes 30724
  431.1 2.0 copy-start.3
  465.6 3.5 copy-start.22
  465.6 3.5 copy-start.24
  470.5 1.8 copy-start.32
  470.5 1.8 copy-start.33
  474.7 293.8 %all-to-all-start = ((f32[16,128,128]{2,1,0:T(8,128)}), f32[16,128,128]{2,1,0:T(8,128)}, u32[]{:S(2)}, u32[]{:S(2)}) async-start(f32[16,128,128]{2,1,0:T(8,128)} %select_select_fusion), calls=%async_computation | async-start | bytes 2097152 | tf_op jit(solution)/shard_map/all_to_all | solution.py:177
  484.4 53.7 %all-reduce.20.cloned.1.call-start = ((), (), s32[]{:S(2)}) async-start(), calls=%async_computation.2 | async-start | bytes 458752 | tf_op jit(solution)/shard_map/psum | solution.py:98
  485.7 166.3 %all-reduce.24.cloned.1.call-start = ((), (), s32[]{:S(2)}) async-start(), calls=%async_computation.4 | async-start | bytes 327680
  494.4 45.8 %copy-start.29 = (s32[6]{0:T(128)S(1)}, s32[6]{0:T(128)}, u32[]{:S(2)}) copy-start(s32[6]{0:T(128)} %fusion.72) | copy-start | bytes 76
  494.4 157.6 %copy-start.7 = (bf16[8,640]{1,0:T(8,128)(2,1)S(1)}, bf16[8,640]{1,0:T(8,128)(2,1)}, u32[]{:S(2)}) copy-start(bf16[8,640]{1,0:T(8,128)(2,1)} %copy-done.6) | copy-start | bytes 30724
  540.1 113.8 %copy-start.13 = (bf16[8,640]{1,0:T(8,128)(2,1)S(1)}, bf16[8,640]{1,0:T(8,128)(2,1)}, u32[]{:S(2)}) copy-start(bf16[8,640]{1,0:T(8,128)(2,1)} %copy-done.12) | copy-start | bytes 30724
  540.1 114.5 %copy-start.28 = (f32[128]{0:T(128)S(1)}, f32[128]{0:T(128)}, u32[]{:S(2)}) copy-start(f32[128]{0:T(128)} %get-tuple-element.28) | copy-start | bytes 1540
  540.1 137.6 %copy-start.27 = (f32[128]{0:T(128)S(1)}, f32[128]{0:T(128)}, u32[]{:S(2)}) copy-start(f32[128]{0:T(128)} %copy-done.26) | copy-start | bytes 1540
  540.1 227.0 %copy-start.9 = (bf16[1,2,8,640]{3,2,1,0:T(8,128)(2,1)S(1)}, bf16[1,2,8,640]{3,2,1,0:T(8,128)(2,1)}, u32[]{:S(2)}) copy-start(bf16[1,2,8,640]{3,2,1,0:T(8,128)(2,1)} %param.21) | copy-start | bytes 61444
  540.1 227.8 %copy-start.11 = (bf16[8,640]{1,0:T(8,128)(2,1)S(1)}, bf16[8,640]{1,0:T(8,128)(2,1)}, u32[]{:S(2)}) copy-start(bf16[8,640]{1,0:T(8,128)(2,1)} %copy-done.10) | copy-start | bytes 30724
  540.2 226.9 %all-reduce.28.cloned.1.call-start = ((), (), s32[]{:S(2)}) async-start(), calls=%async_computation.6 | async-start | bytes 655360
  652.7 117.6 %copy-start.4 = (f32[1,1,1,6,128,128]{5,4,3,2,1,0:T(8,128)S(1)}, f32[1,1,1,6,128,128]{5,4,3,2,1,0:T(8,128)}, u32[]{:S(2)}) copy-start(f32[1,1,1,6,128,128]{5,4,3,2,1,0:T(8,128)} %param.28) | copy-start | bytes 1179652
  652.7 117.6 %copy-start.5 = (f32[1,1,1,6,128,128]{5,4,3,2,1,0:T(8,128)S(1)}, f32[1,1,1,6,128,128]{5,4,3,2,1,0:T(8,128)}, u32[]{:S(2)}) copy-start(f32[1,1,1,6,128,128]{5,4,3,2,1,0:T(8,128)} %param.29) | copy-start | bytes 1179652
  652.7 117.6 %copy-start.30 = (pred[6]{0:T(512)(128)(4,1)S(1)}, pred[6]{0:T(512)(128)(4,1)}, u32[]{:S(2)}) copy-start(pred[6]{0:T(512)(128)(4,1)} %fusion.65) | copy-start | bytes 22
  652.7 117.6 %copy-start.31 = (pred[6]{0:T(512)(128)(4,1)S(1)}, pred[6]{0:T(512)(128)(4,1)}, u32[]{:S(2)}) copy-start(pred[6]{0:T(512)(128)(4,1)} %compare_and_fusion.3) | copy-start | bytes 22
Sparse Core Ops, SparseCore 0:
  68.2 51.6 all-reduce.31
  122.8 115.7 all-reduce.25
  241.6 49.1 all-reduce.17
  293.5 110.9 all-reduce.21
  406.9 53.0 all-reduce.29
  487.9 50.0 all-reduce.19
  541.0 110.9 all-reduce.23
  655.0 112.0 all-reduce.27
where the time goes:
time: 779 us; the launch traced here: 778 us
  waiting for transfers between devices  507 us (65%)
  blocking collectives  185 us (24%)
  other arithmetic  22 us (3%)
  local copies, waits for them, and re-layouts  18.4 us (2%)
  between operations  16 us (2%)
  matrix products  15.5 us (2%)
  starting transfers between devices  14.6 us (2%)
    unnamed x12, waiting for transfers between devices  359 us
    psum x2, waiting for transfers between devices, body(): lax.psum(forward_product.astype(jnp.bfloat16), 'tensor').astype(jnp.float32)  93.6 us
    psum x2, waiting for transfers between devices, body(): lax.psum((product, squares, act_grad), 'tensor')  53.8 us
    unnamed x2, blocking collectives  51.2 us
    all_gather x2, blocking collectives, body(): rows_all = lax.all_gather(rows_local, 'dp', axis=0, tiled=True)  41.1 us
    all_gather x2, blocking collectives, body(): grads_all = lax.all_gather(grads_in, 'dp', axis=0, tiled=True)  36.3 us
    all_gather x2, blocking collectives, body(): forward_rows_all = lax.all_gather(rows_in, 'dp', axis=0, tiled=True)  31.2 us
    psum x2, blocking collectives, body(): lax.psum(forward_squares.astype(jnp.bfloat16), 'tensor').astype(jnp.float32)  16.6 us
  transfers between devices with their start and end apart: 11, of which 8 were waited for; matrix products, arithmetic and copies ran while one was open for 4% of the time, Pallas kernels for 0%

commit v1 on v0

--- a/solution.py
+++ b/solution.py
@@ -1,3 +1,4 @@
+import functools
 import jax
 import jax.numpy as jnp
 from jax import lax
@@ -6,6 +7,25 @@
 DW = 2560
 BLK = 128
 EPSILON = 1e-06
+
+
+def put_the_tables(values, at_axis):
+    vals = [values]
+    axis_len = jax.lax.axis_size("dp")
+    for b in range(axis_len - 1):
+        vals.append(
+            jax.lax.ppermute(
+                vals[-1], axis_name="dp", perm=[(p, (p + 1) % axis_len) for p in range(axis_len)]
+            )
+        )
+    return jnp.roll(
+        jnp.concatenate(vals[::-1], at_axis),
+        (jax.lax.axis_index("dp") + 1) * values.shape[at_axis],
+        at_axis,
+    )
+
+
+shapes_measure = functools.partial(put_the_tables, at_axis=0)
 
 
 def from_behind(value, axis, steps):
@@ -123,7 +143,7 @@
             grads_in = jnp.where(section_index == section_count - 1, masked, passed_grads)
         rows_local = stashed_inputs[0, turn]
         rows_all = lax.all_gather(rows_local, "dp", axis=0, tiled=True)
-        grads_all = lax.all_gather(grads_in, "dp", axis=0, tiled=True)
+        grads_all = shapes_measure(grads_in)
         normed, squares, product = normed_product(rows_all, gain_row, up_matrix)
         act_grad = times_transposed(grads_all, down_matrix)
         product, squares, act_grad = lax.psum((product, squares, act_grad), "tensor")

time: 779 us -> 833 us (1.069)
  waiting for transfers between devices: 507 us -> 585 us
  blocking collectives: 185 us -> 143 us
  starting transfers between devices: 14.6 us -> 26.9 us
    ppermute x0 -> x30, waiting for transfers between devices: none -> 96.9 us  [put_the_tables(): jax.lax.ppermute(vals[-1], axis_name='dp', perm=[(p, (p + 1) % axis_len)...]
    psum x2, waiting for transfers between devices: 93.6 us -> 43.6 us  [body(): lax.psum(forward_product.astype(jnp.bfloat16), 'tensor').astype(jnp.float32)]
    all_gather x2 -> x0, blocking collectives: 36.3 us -> none  [body(): grads_all = lax.all_gather(grads_in, 'dp', axis=0, tiled=True)]
    unnamed x12, waiting for transfers between devices: 359 us -> 388 us
    ppermute x0 -> x30, starting transfers between devices: none -> 12.5 us  [put_the_tables(): jax.lax.ppermute(vals[-1], axis_name='dp', perm=[(p, (p + 1) % axis_len)...]
  transfers between devices with their start and end apart: 11 -> 41, of which waited for: 8 -> 35; matrix products, arithmetic and copies ran while one was open for 4% -> 4% of each run, Pallas kernels for 0% -> 0%
where the time goes in v1:
time: 833 us; the launch traced here: 832 us
  waiting for transfers between devices  585 us (70%)
  blocking collectives  143 us (17%)
  starting transfers between devices  26.9 us (3%)
  other arithmetic  23.6 us (3%)
  local copies, waits for them, and re-layouts  20.8 us (2%)
  matrix products  16.5 us (2%)
  between operations  16 us (2%)
    unnamed x12, waiting for transfers between devices  388 us
    ppermute x30, waiting for transfers between devices, put_the_tables(): jax.lax.ppermute(vals[-1], axis_name='dp', perm=[(p, (p + 1) % axis_len)...  96.9 us
    psum x2, waiting for transfers between devices, body(): lax.psum((product, squares, act_grad), 'tensor')  53.5 us
    unnamed x2, blocking collectives  49.5 us
    psum x2, waiting for transfers between devices, body(): lax.psum(forward_product.astype(jnp.bfloat16), 'tensor').astype(jnp.float32)  43.6 us
    all_gather x2, blocking collectives, body(): forward_rows_all = lax.all_gather(rows_in, 'dp', axis=0, tiled=True)  34.3 us
    all_gather x2, blocking collectives, body(): rows_all = lax.all_gather(rows_local, 'dp', axis=0, tiled=True)  33.2 us
    psum x2, blocking collectives, body(): lax.psum(forward_squares.astype(jnp.bfloat16), 'tensor').astype(jnp.float32)  16.9 us
  transfers between devices with their start and end apart: 41, of which 35 were waited for; matrix products, arithmetic and copies ran while one was open for 4% of the time, Pallas kernels for 0%

profile of v1, /device:TPU:1, one launch (start us, length us, event | category | flops | bytes accessed | tf_op | source)
XLA Modules:
  0.0 832.3 jit_solution(2538199378248659921)
XLA Ops:
  7.2 3.5 collective-permute-start.1
  10.7 4.3 collective-permute-done.1
  15.0 4.5 collective-permute-done.2
  19.5 4.3 collective-permute-done.3
  23.8 4.3 collective-permute-done.4
  28.1 4.3 collective-permute-done.5
  32.4 4.3 collective-permute-done.6
  36.7 4.3 collective-permute-done.7
  41.0 4.3 collective-permute-done.8
  45.3 4.3 collective-permute-done.9
  50.4 3.6 collective-permute-done.10
  54.6 3.6 collective-permute-done.11
  58.3 18.1 %all-gather.1 = bf16[1,1,128,640]{3,2,1,0:T(8,128)(2,1)S(1)} all-gather(bf16[1,1,8,640]{3,2,1,0:T(8,128)(2,1)S(1)} %get-tuple-element.42), channel_id=3, replica_groups=mesh['section'=8,'dp'=16,'tensor'=4] {'dp'}, dimensions={2}, use_global_device_ids=true | all-gather | bytes 174080 | tf_op jit(solution)/shard_map/all_gather | solution.py:145
  76.3 1.9 collective-permute-start.13
  78.2 15.2 %all-gather.2 = bf16[1,1,128,640]{3,2,1,0:T(8,128)(2,1)S(1)} all-gather(bf16[1,1,8,640]{3,2,1,0:T(8,128)(2,1)S(1)} %get-tuple-element.43), channel_id=4, replica_groups=mesh['section'=8,'dp'=16,'tensor'=4] {'dp'}, dimensions={2}, use_global_device_ids=true | all-gather | bytes 174080 | tf_op jit(solution)/shard_map/all_gather | solution.py:145
  94.9 1.9 collective-permute-start.15
  100.5 18.1 %all-gather = bf16[1,128,640]{2,1,0:T(8,128)(2,1)S(1)} all-gather(bf16[1,8,640]{2,1,0:T(8,128)(2,1)S(1)} %copy-done.9), channel_id=2, replica_groups=mesh['section'=8,'dp'=16,'tensor'=4] {'dp'}, dimensions={1}, use_global_device_ids=true | all-gather | bytes 174080 | tf_op jit(solution)/shard_map/all_gather | solution.py:113
  118.8 9.3 %all-reduce.6 = (f32[128]{0:T(128)S(1)}, f32[128]{0:T(128)S(1)}) all-reduce(f32[128]{0:T(128)S(1)} %get-tuple-element.39, f32[128]{0:T(128)S(1)} %get-tuple-element.44), channel_id=1, replica_groups=mesh['section'=8,'dp'=16,'tensor'=4] {'tensor'}, use_global_device_ids=true, to_apply=%region_18.20 | all-reduce | flops 256 | bytes 2048 | tf_op jit(solution)/shard_map/psum | solution.py:149
  128.0 28.9 %all-reduce.32.cloned.1.call-done = (f32[128,896]{1,0:T(8,128)}, f32[128,896]{1,0:T(8,128)}) async-done(((f32[128,896]{1,0:T(8,128)}, f32[128,896]{1,0:T(8,128)}), (f32[128,896]{1,0:T(8,128)}, f32[128,896]{1,0:T(8,128)})) %all-reduce.32.cloned.1.call-update) | async-done | bytes 917520 | tf_op jit(solution)/shard_map/psum | solution.py:149
  156.9 2.2 multiply_reduce_fusion.1
  160.4 1.3 convolution_convert_fusion.1
  164.7 1.3 dynamic-slice.1
  167.3 26.3 %all-reduce.3 = f32[128]{0:T(128)S(1)} all-reduce(f32[128]{0:T(128)S(1)} %get-tuple-element.31), channel_id=8, replica_groups=mesh['section'=8,'dp'=16,'tensor'=4] {'dp'}, use_global_device_ids=true, to_apply=%region_14.16.clone | all-reduce | flops 128 | bytes 1024
  193.7 82.5 %all-reduce.26.cloned.1.call-done = f32[128,640]{1,0:T(8,128)} async-done(((f32[128,640]{1,0:T(8,128)}), f32[128,640]{1,0:T(8,128)}) %all-reduce.26.cloned.1.call-update) | async-done | bytes 327696
  276.9 1.3 collective-permute-start.16
  278.2 3.1 collective-permute-done.16
  281.4 1.3 collective-permute-start.17
  283.7 2.1 collective-permute-start.18
  285.8 2.2 collective-permute-done.18
  289.0 3.3 collective-permute-done.19
  292.9 3.7 collective-permute-done.20
  297.2 3.8 collective-permute-done.21
  301.5 3.7 collective-permute-done.22
  305.4 8.4 %psum.71 = bf16[128]{0:T(256)(128)(2,1)S(1)} all-reduce(bf16[128]{0:T(256)(128)(2,1)S(1)} %fusion.21), channel_id=1, replica_groups=mesh['section'=8,'dp'=16,'tensor'=4] {'tensor'}, use_global_device_ids=true, to_apply=%region_2.3 | all-reduce | flops 128 | bytes 512 | tf_op jit(solution)/shard_map/psum | solution.py:119
  314.6 5.5 collective-permute-done.24
  320.2 4.2 collective-permute-done.25
  324.4 4.3 collective-permute-done.26
  329.4 3.7 collective-permute-done.27
  333.1 4.3 collective-permute-done.28
  338.0 3.7 collective-permute-done.29
  342.2 3.8 collective-permute-done.30
  346.0 2.0 convolution_convert_fusion.3
  348.1 2.2 collective-permute-done.31
  351.3 1.3 fusion
  352.5 104.4 %all-reduce.22.cloned.1.call-done = bf16[128,640]{1,0:T(8,128)(2,1)} async-done(((bf16[128,640]{1,0:T(8,128)(2,1)}), bf16[128,640]{1,0:T(8,128)(2,1)}) %all-reduce.22.cloned.1.call-update) | async-done | bytes 163856
  457.7 3.1 collective-permute-start
  463.9 16.2 %all_gather.13 = bf16[128,640]{1,0:T(8,128)(2,1)S(1)} all-gather(bf16[8,640]{1,0:T(8,128)(2,1)S(1)} %bitcast_select_fusion.2), channel_id=1, replica_groups=mesh['section'=8,'dp'=16,'tensor'=4] {'dp'}, dimensions={0}, use_global_device_ids=true | all-gather | bytes 174080 | tf_op jit(solution)/shard_map/all_gather | solution.py:113
  482.0 1.3 gather_fusion.2
  485.5 1.4 fusion.32
  487.9 24.6 %all-reduce.30.cloned.1.call-done = (f32[128,896]{1,0:T(8,128)}, f32[128,896]{1,0:T(8,128)}) async-done(((f32[128,896]{1,0:T(8,128)}, f32[128,896]{1,0:T(8,128)}), (f32[128,896]{1,0:T(8,128)}, f32[128,896]{1,0:T(8,128)})) %all-reduce.30.cloned.1.call-update) | async-done | bytes 917520 | tf_op jit(solution)/shard_map/psum | solution.py:149
  512.5 2.1 multiply_reduce_fusion
  515.4 1.8 copy.151
  522.8 1.4 convolution_add_fusion
  524.2 1.9 gather_fusion
  526.1 2.5 select_select_fusion
  528.5 9.7 %all-to-all-start = ((f32[16,128,128]{2,1,0:T(8,128)}), f32[16,128,128]{2,1,0:T(8,128)}, u32[]{:S(2)}, u32[]{:S(2)}) async-start(f32[16,128,128]{2,1,0:T(8,128)} %select_select_fusion), calls=%async_computation | async-start | bytes 2097152 | tf_op jit(solution)/shard_map/all_to_all | solution.py:197
  539.7 8.5 %psum.73 = bf16[128]{0:T(256)(128)(2,1)S(1)} all-reduce(bf16[128]{0:T(256)(128)(2,1)S(1)} %fusion.19), channel_id=1, replica_groups=mesh['section'=8,'dp'=16,'tensor'=4] {'tensor'}, use_global_device_ids=true, to_apply=%region_6.7 | all-reduce | flops 128 | bytes 512 | tf_op jit(solution)/shard_map/psum | solution.py:119
  548.3 43.6 %all-reduce.20.cloned.1.call-done = bf16[128,896]{1,0:T(8,128)(2,1)} async-done(((bf16[128,896]{1,0:T(8,128)(2,1)}), bf16[128,896]{1,0:T(8,128)(2,1)}) %all-reduce.20.cloned.1.call-update) | async-done | bytes 229392 | tf_op jit(solution)/shard_map/psum | solution.py:118
  591.9 2.0 convolution_convert_fusion.2
  594.0 111.8 %all-reduce.24.cloned.1.call-done = bf16[128,640]{1,0:T(8,128)(2,1)} async-done(((bf16[128,640]{1,0:T(8,128)(2,1)}), bf16[128,640]{1,0:T(8,128)(2,1)}) %all-reduce.24.cloned.1.call-update) | async-done | bytes 163856
  708.4 23.2 %all-reduce.5 = f32[128]{0:T(128)S(1)} all-reduce(f32[128]{0:T(128)S(1)} %copy-done.16), channel_id=10, replica_groups=mesh['section'=8,'dp'=16,'tensor'=4] {'dp'}, use_global_device_ids=true, to_apply=%region_21.23.clone | all-reduce | flops 128 | bytes 1024
  731.6 89.3 %all-reduce.28.cloned.1.call-done = f32[128,640]{1,0:T(8,128)} async-done(((f32[128,640]{1,0:T(8,128)}), f32[128,640]{1,0:T(8,128)}) %all-reduce.28.cloned.1.call-update) | async-done | bytes 327696
  822.3 1.8 gather_fusion.1
  824.2 1.3 divide_select_fusion
  (201 shorter events, 40.4 us)
Async XLA Ops:
  7.2 89.6 %copy-start = (bf16[1,640,896]{2,1,0:T(8,128)(2,1)S(1)}, bf16[1,640,896]{2,1,0:T(8,128)(2,1)}, u32[]{:S(2)}) copy-start(bf16[1,640,896]{2,1,0:T(8,128)(2,1)} %param.25) | copy-start | bytes 3440644
  7.2 149.8 %all-reduce.32.cloned.1.call-start = ((), (), s32[]{:S(2)}) async-start(), calls=%async_computation.8 | async-start | bytes 1835008 | tf_op jit(solution)/shard_map/psum | solution.py:149
  7.2 7.8 collective-permute-start.1
  15.0 4.5 collective-permute-start.2
  19.5 4.3 collective-permute-start.3
  23.8 4.3 collective-permute-start.4
  28.1 4.3 collective-permute-start.5
  32.4 4.3 collective-permute-start.6
  36.7 4.3 collective-permute-start.7
  41.0 4.3 collective-permute-start.8
  45.3 4.3 collective-permute-start.9
  49.6 4.3 collective-permute-start.10
  53.9 4.3 collective-permute-start.11
  58.2 18.1 %collective-permute-start.12 = (bf16[8,640]{1,0:T(8,128)(2,1)S(1)}, bf16[8,640]{1,0:T(8,128)(2,1)S(1)}, u32[]{:S(2)}, u32[]{:S(2)}) collective-permute-start(bf16[8,640]{1,0:T(8,128)(2,1)S(1)} %collective-permute-done.11), channel_id=1, source_target_pairs={{0,4},{4,8},{8,12},{12,16},{16,20},{20,24},{24,28},{28,32},{32,36}... | collective-permute-start | bytes 30728 | tf_op jit(solution)/shard_map/ppermute | solution.py:17
  76.3 17.4 %collective-permute-start.13 = (bf16[8,640]{1,0:T(8,128)(2,1)S(1)}, bf16[8,640]{1,0:T(8,128)(2,1)S(1)}, u32[]{:S(2)}, u32[]{:S(2)}) collective-permute-start(bf16[8,640]{1,0:T(8,128)(2,1)S(1)} %collective-permute-done.12), channel_id=1, source_target_pairs={{0,4},{4,8},{8,12},{12,16},{16,20},{20,24},{24,28},{28,32},{32,36}... | collective-permute-start | bytes 30728 | tf_op jit(solution)/shard_map/ppermute | solution.py:17
  93.7 1.2 collective-permute-start.14
  93.9 5.1 copy-start.8
  94.9 4.0 collective-permute-start.15
  96.8 2.4 copy-start.1
  99.2 1.3 copy-start.9
  100.5 175.7 %all-reduce.26.cloned.1.call-start = ((), (), s32[]{:S(2)}) async-start(), calls=%async_computation.5 | async-start | bytes 655360
  160.3 1.4 copy-start.10
  160.3 3.2 copy-start.22
  160.3 3.2 copy-start.14
  160.3 185.7 %all-reduce.18.cloned.1.call-start = ((), (), s32[]{:S(2)}) async-start(), calls=%async_computation.1 | async-start | bytes 458752 | tf_op jit(solution)/shard_map/psum | solution.py:118
  161.6 114.5 %copy-start.7 = (bf16[1,2,8,640]{3,2,1,0:T(8,128)(2,1)S(1)}, bf16[1,2,8,640]{3,2,1,0:T(8,128)(2,1)}, u32[]{:S(2)}) copy-start(bf16[1,2,8,640]{3,2,1,0:T(8,128)(2,1)} %param.23) | copy-start | bytes 61444
  161.6 119.7 %copy-start.11 = (bf16[1,8,640]{2,1,0:T(8,128)(2,1)S(1)}, bf16[1,8,640]{2,1,0:T(8,128)(2,1)}, u32[]{:S(2)}) copy-start(bf16[1,8,640]{2,1,0:T(8,128)(2,1)} %param.21) | copy-start | bytes 30724
  161.7 295.3 %all-reduce.22.cloned.1.call-start = ((), (), s32[]{:S(2)}) async-start(), calls=%async_computation.3 | async-start | bytes 327680
  276.9 4.4 collective-permute-start.16
  281.4 2.3 collective-permute-start.17
  283.7 4.3 collective-permute-start.18
  288.0 4.3 collective-permute-start.19
  292.3 4.3 collective-permute-start.20
  296.6 4.3 collective-permute-start.21
  301.0 4.3 collective-permute-start.22
  305.3 8.5 %collective-permute-start.23 = (bf16[8,640]{1,0:T(8,128)(2,1)S(1)}, bf16[8,640]{1,0:T(8,128)(2,1)S(1)}, u32[]{:S(2)}, u32[]{:S(2)}) collective-permute-start(bf16[8,640]{1,0:T(8,128)(2,1)S(1)} %collective-permute-done.22), channel_id=1, source_target_pairs={{0,4},{4,8},{8,12},{12,16},{16,20},{20,24},{24,28},{28,32},{32,36}... | collective-permute-start | bytes 30728 | tf_op jit(solution)/shard_map/ppermute | solution.py:17
  313.8 6.3 collective-permute-start.24
  320.1 4.3 collective-permute-start.25
  324.4 4.3 collective-permute-start.26
  328.7 4.3 collective-permute-start.27
  333.0 4.3 collective-permute-start.28
  337.4 4.3 collective-permute-start.29
  341.7 4.3 collective-permute-start.30
  346.0 4.3 collective-permute-start.31
  348.0 164.4 %all-reduce.30.cloned.1.call-start = ((), (), s32[]{:S(2)}) async-start(), calls=%async_computation.7 | async-start | bytes 1835008 | tf_op jit(solution)/shard_map/psum | solution.py:149
  350.6 0.7 copy-start.2
  352.5 111.4 %copy-start.12 = (bf16[1,8,640]{2,1,0:T(8,128)(2,1)S(1)}, bf16[1,8,640]{2,1,0:T(8,128)(2,1)}, u32[]{:S(2)}) copy-start(bf16[1,8,640]{2,1,0:T(8,128)(2,1)} %param.19) | copy-start | bytes 30724
  457.7 6.2 collective-permute-start
  461.3 19.2 %copy-start.4 = (bf16[128,896]{1,0:T(8,128)(2,1)S(1)}, bf16[128,896]{1,0:T(8,128)(2,1)}, u32[]{:S(2)}) copy-start(bf16[128,896]{1,0:T(8,128)(2,1)} %get-tuple-element.37) | copy-start | bytes 688132
  483.3 3.6 copy-start.3
  519.5 3.3 copy-start.13
  524.2 1.9 copy-start.20
  524.2 1.9 copy-start.21
  528.5 293.8 %all-to-all-start = ((f32[16,128,128]{2,1,0:T(8,128)}), f32[16,128,128]{2,1,0:T(8,128)}, u32[]{:S(2)}, u32[]{:S(2)}) async-start(f32[16,128,128]{2,1,0:T(8,128)} %select_select_fusion), calls=%async_computation | async-start | bytes 2097152 | tf_op jit(solution)/shard_map/all_to_all | solution.py:197
  538.2 53.7 %all-reduce.20.cloned.1.call-start = ((), (), s32[]{:S(2)}) async-start(), calls=%async_computation.2 | async-start | bytes 458752 | tf_op jit(solution)/shard_map/psum | solution.py:118
  539.6 166.3 %all-reduce.24.cloned.1.call-start = ((), (), s32[]{:S(2)}) async-start(), calls=%async_computation.4 | async-start | bytes 327680
  548.3 45.8 %copy-start.17 = (s32[6]{0:T(128)S(1)}, s32[6]{0:T(128)}, u32[]{:S(2)}) copy-start(s32[6]{0:T(128)} %fusion.75) | copy-start | bytes 76
  593.9 114.5 %copy-start.16 = (f32[128]{0:T(128)S(1)}, f32[128]{0:T(128)}, u32[]{:S(2)}) copy-start(f32[128]{0:T(128)} %get-tuple-element.29) | copy-start | bytes 1540
  593.9 137.6 %copy-start.15 = (f32[128]{0:T(128)S(1)}, f32[128]{0:T(128)}, u32[]{:S(2)}) copy-start(f32[128]{0:T(128)} %add_rsqrt_fusion) | copy-start | bytes 1540
  594.0 227.0 %all-reduce.28.cloned.1.call-start = ((), (), s32[]{:S(2)}) async-start(), calls=%async_computation.6 | async-start | bytes 655360
  706.5 117.6 %copy-start.5 = (f32[1,1,1,6,128,128]{5,4,3,2,1,0:T(8,128)S(1)}, f32[1,1,1,6,128,128]{5,4,3,2,1,0:T(8,128)}, u32[]{:S(2)}) copy-start(f32[1,1,1,6,128,128]{5,4,3,2,1,0:T(8,128)} %param.30) | copy-start | bytes 1179652
  706.5 117.6 %copy-start.6 = (f32[1,1,1,6,128,128]{5,4,3,2,1,0:T(8,128)S(1)}, f32[1,1,1,6,128,128]{5,4,3,2,1,0:T(8,128)}, u32[]{:S(2)}) copy-start(f32[1,1,1,6,128,128]{5,4,3,2,1,0:T(8,128)} %param.31) | copy-start | bytes 1179652
  706.5 117.6 %copy-start.18 = (pred[6]{0:T(512)(128)(4,1)S(1)}, pred[6]{0:T(512)(128)(4,1)}, u32[]{:S(2)}) copy-start(pred[6]{0:T(512)(128)(4,1)} %compare_and_fusion.3) | copy-start | bytes 22
  706.6 117.6 %copy-start.19 = (pred[6]{0:T(512)(128)(4,1)S(1)}, pred[6]{0:T(512)(128)(4,1)}, u32[]{:S(2)}) copy-start(pred[6]{0:T(512)(128)(4,1)} %fusion.67) | copy-start | bytes 22
Sparse Core Ops, SparseCore 0:
  100.6 56.3 all-reduce.31
  160.4 115.6 all-reduce.25
  279.1 49.1 all-reduce.17
  348.2 108.7 all-reduce.21
  459.3 53.0 all-reduce.29
  541.8 50.0 all-reduce.19
  594.8 110.9 all-reduce.23
  708.8 112.0 all-reduce.27
